TPU v7x, 32 devices: a whole 2x2x4 slice. The times are simulated.
32 devices in a mesh: dom: 8 (over z, core), rep: 4 (over y, x).
Axes of the slice: x: 2, y: 2, z: 4, core: 2. Of those that a mesh axis runs over, the one named last changes fastest.
Arguments:
- node_features: bfloat16 [16384, 256], P(('dom', 'rep')), may hold values from -6 to 6
- weight: bfloat16 [256, 256], replicated, may hold values from -0.375 to 0.375
- cotangent: bfloat16 [16384, 256], P(('dom', 'rep')), may hold values from -6 to 6
- tile_row: int32 [8, 4, 512], P('dom', 'rep'), may hold values from 0 to 15
- tile_col: int32 [8, 4, 512], P('dom', 'rep'), may hold values from 0 to 31
- tile_values: bfloat16 [8, 4, 512, 128, 128], P('dom', 'rep'), may hold values from -0.0625 to 0.0625
- tile_count: int32 [8, 4], P('dom', 'rep'), may hold values from 128 to 512, as said below
Outputs:
- output: bfloat16 [16384, 256], P(('dom', 'rep'))
- grad_features: bfloat16 [16384, 256], P(('dom', 'rep'))
- grad_weight: float32 [256, 256], replicated
Inputs may be any that keep to these rules, and one draw needn't show every extreme that they name: Live slots are the first tile_count slots of each device's list; some device has all 512 slots live.
All inputs are finite; a program needn't handle non-finite values.
Results may differ from a plain program's by a relative error of at most 0.0061.
Values may be sent and summed in bfloat16 or wider, within the bound.
A program may use at most 192 MiB of HBM per device.

v0:
```python
import jax
import jax.numpy as jnp
from jax import lax
from jax.sharding import PartitionSpec as P


def silu_slope(summed):
    sig = jax.nn.sigmoid(summed)
    return sig * (1.0 + summed * (1.0 - sig))


def tile_products(values, pick_index, place_index, active, source, out_blocks, flipped):
    slots = values.shape[0]
    feature_width = source.shape[2]
    per_turn = min(slots, 128)
    pattern = "tba,tbf->taf" if flipped else "tab,tbf->taf"

    def accumulate(turn_index, summed):
        first_slot = turn_index * per_turn
        block_values = lax.dynamic_slice_in_dim(values, first_slot, per_turn, 0)
        picks = lax.dynamic_slice_in_dim(pick_index, first_slot, per_turn, 0)
        picked = jnp.take(source, picks, axis=0)
        products = jnp.einsum(pattern, block_values, picked, preferred_element_type=jnp.float32)
        places = lax.dynamic_slice_in_dim(place_index, first_slot, per_turn, 0)
        enabled = lax.dynamic_slice_in_dim(active, first_slot, per_turn, 0)
        products = products * enabled.astype(jnp.float32)[:, None, None]
        return summed.at[places].add(products)

    initial = jnp.zeros((out_blocks, 128, feature_width), jnp.float32)
    summed = lax.fori_loop(0, slots // per_turn, accumulate, initial)
    return summed.reshape(out_blocks * 128, feature_width)


def body(node_features, weight, cotangent, tile_row, tile_col, tile_values, tile_count):
    rows_here = node_features.shape[0]
    feature_width = weight.shape[0]
    dom_size = lax.axis_size("dom")
    rep_size = lax.axis_size("rep")
    slots = tile_row.shape[2]
    row_index = tile_row.reshape(slots)
    col_index = tile_col.reshape(slots)
    values = tile_values.reshape(slots, 128, 128)
    active = lax.broadcasted_iota(jnp.int32, (slots,), 0) < tile_count.reshape(())
    raw_rows = lax.all_gather(node_features, "dom", axis=0, tiled=True)
    gathered = jnp.dot(raw_rows, weight, preferred_element_type=jnp.float32).astype(jnp.bfloat16)
    source = gathered.reshape(-1, 128, feature_width)
    part_blocks = rep_size * rows_here // 128
    partial_value = tile_products(values, col_index, row_index, active, source, part_blocks, False)
    summed = lax.psum_scatter(partial_value, "rep", scatter_dimension=0, tiled=True)
    output = jax.nn.silu(summed).astype(jnp.bfloat16)
    grad_own = (cotangent.astype(jnp.float32) * silu_slope(summed)).astype(jnp.bfloat16)
    grad_block = lax.all_gather(grad_own, "rep", axis=0, tiled=True)
    back_blocks = dom_size * rows_here // 128
    back_partial = tile_products(
        values,
        row_index,
        col_index,
        active,
        grad_block.reshape(-1, 128, feature_width),
        back_blocks,
        True,
    )
    grad_projected = lax.psum_scatter(back_partial, "dom", scatter_dimension=0, tiled=True).astype(
        jnp.bfloat16
    )
    grad_features = jnp.dot(grad_projected, weight.T, preferred_element_type=jnp.float32).astype(
        jnp.bfloat16
    )
    local_weight = jnp.dot(node_features.T, grad_projected, preferred_element_type=jnp.float32)
    grad_weight = lax.psum(local_weight, ("dom", "rep"))
    return (output, grad_features, grad_weight)


def solution(mesh):
    placed = (
        P(("dom", "rep"), None),
        P(),
        P(("dom", "rep"), None),
        P("dom", "rep", None),
        P("dom", "rep", None),
        P("dom", "rep", None, None, None),
        P("dom", "rep"),
    )
    return jax.shard_map(
        body,
        mesh=mesh,
        in_specs=placed,
        out_specs=(P(("dom", "rep"), None), P(("dom", "rep"), None), P()),
        check_vma=False,
    )
```

profile of v0, /device:TPU:0, one launch (start us, length us, event | category | flops | bytes accessed | tf_op | source)
XLA Modules:
  0.0 719.0 jit_solution(10474179831010498034)
XLA Ops:
  7.2 0.0 all-gather.3.cloned.1.call-start
  7.2 0.7 all-gather.3.cloned.1.call-update
  7.9 0.0 reduce-scatter.3.cloned.1.call-start
  8.6 32.9 %all-gather.3.cloned.1.call-done = bf16[4096,256]{1,0:T(8,128)(2,1)} async-done(((bf16[512,256]{1,0:T(8,128)(2,1)}), bf16[4096,256]{1,0:T(8,128)(2,1)}) %all-gather.3.cloned.1.call-update) | async-done | bytes 2097168 | tf_op jit(solution)/shard_map/all_gather | solution.py:44
  41.5 3.7 convolution_convert_fusion
  45.2 0.2 broadcast_in_dim.74
  45.4 181.9 %while.26 = (s32[]{:T(128)}, f32[16,128,256]{2,1,0:T(8,128)S(1)}, s32[512]{0:T(512)S(1)}, bf16[512,128,128]{2,1,0:T(8,128)(2,1)}, s32[512]{0:T(512)S(1)}, /*inde...) while((s32[]{:T(128)}, f32[16,128,256]{2,1,0:T(8,128)S(1)}, ...), condition=%wide.region_2.3_spmd, body=%wide.region_0.2_spmd.sunk | while | flops 1086327040 | bytes 96478248 | solution.py:30
  45.4 0.1 compare_and_fusion.4
  45.5 8.2 %gather_fusion = bf16[128,128,256]{2,1,0:T(8,128)(2,1)} fusion(bf16[32,128,256]{2,1,0:T(8,128)(2,1)} %get-tuple-element.424, s32[1024]{0:T(1024)S(1)} %pad_clamp_fusion.4), kind=kCustom, calls=%fused_computation.clone.1 | custom fusion | bytes 16777728 | tf_op jit(solution)/shard_map/while/body/eval_jaxpr/jit(_take)/gather | solution.py:22
  53.7 12.8 %convolution_multiply_fusion.4 = f32[128,128,256]{2,1,0:T(8,128)} fusion(f32[128]{0:T(128)S(1)} %get-tuple-element.384, bf16[128,128,256]{2,1,0:T(8,128)(2,1)} %gather_fusion, pred[128]{0:T(512)(128)(4,1)S(1)} %get-tuple-element.386, bf16[512,128,128]{2,1,0:T(8,128)(2,1)} %get-tuple-element.422, s32[]{:T(128)S(6)} %select_n.85), kind=kOutput, calls=%fused_computation.4.clone.1 | convolution fusion | flops 1082130432 | bytes 29360772 | tf_op jit(solution)/shard_map/while/body/eval_jaxpr/tab,tbf->taf/dot_general | solution.py:23
  66.5 0.1 compare_select_fusion.8
  66.6 24.3 %scatter_fusion = f32[16,128,256]{2,1,0:T(8,128)S(1)} fusion(f32[16,128,256]{2,1,0:T(8,128)S(1)} %get-tuple-element.409, s32[128]{0:T(128)S(1)} %compare_select_fusion.8, f32[128,128,256]{2,1,0:T(8,128)} %convolution_multiply_fusion.4), kind=kCustom, calls=%fused_computation.2.clone.1 | custom fusion | flops 4194304 | bytes 50332160 | tf_op jit(solution)/shard_map/while/body/eval_jaxpr/scatter-add | solution.py:27
  90.9 0.1 compare_and_fusion.4
  91.0 8.2 %gather_fusion = bf16[128,128,256]{2,1,0:T(8,128)(2,1)} fusion(bf16[32,128,256]{2,1,0:T(8,128)(2,1)} %get-tuple-element.424, s32[1024]{0:T(1024)S(1)} %pad_clamp_fusion.4), kind=kCustom, calls=%fused_computation.clone.1 | custom fusion | bytes 16777728 | tf_op jit(solution)/shard_map/while/body/eval_jaxpr/jit(_take)/gather | solution.py:22
  99.2 12.8 %convolution_multiply_fusion.4 = f32[128,128,256]{2,1,0:T(8,128)} fusion(f32[128]{0:T(128)S(1)} %get-tuple-element.384, bf16[128,128,256]{2,1,0:T(8,128)(2,1)} %gather_fusion, pred[128]{0:T(512)(128)(4,1)S(1)} %get-tuple-element.386, bf16[512,128,128]{2,1,0:T(8,128)(2,1)} %get-tuple-element.422, s32[]{:T(128)S(6)} %select_n.85), kind=kOutput, calls=%fused_computation.4.clone.1 | convolution fusion | flops 1082130432 | bytes 29360772 | tf_op jit(solution)/shard_map/while/body/eval_jaxpr/tab,tbf->taf/dot_general | solution.py:23
  112.0 0.1 compare_select_fusion.8
  112.1 24.3 %scatter_fusion = f32[16,128,256]{2,1,0:T(8,128)S(1)} fusion(f32[16,128,256]{2,1,0:T(8,128)S(1)} %get-tuple-element.409, s32[128]{0:T(128)S(1)} %compare_select_fusion.8, f32[128,128,256]{2,1,0:T(8,128)} %convolution_multiply_fusion.4), kind=kCustom, calls=%fused_computation.2.clone.1 | custom fusion | flops 4194304 | bytes 50332160 | tf_op jit(solution)/shard_map/while/body/eval_jaxpr/scatter-add | solution.py:27
  136.4 0.1 compare_and_fusion.4
  136.5 8.2 %gather_fusion = bf16[128,128,256]{2,1,0:T(8,128)(2,1)} fusion(bf16[32,128,256]{2,1,0:T(8,128)(2,1)} %get-tuple-element.424, s32[1024]{0:T(1024)S(1)} %pad_clamp_fusion.4), kind=kCustom, calls=%fused_computation.clone.1 | custom fusion | bytes 16777728 | tf_op jit(solution)/shard_map/while/body/eval_jaxpr/jit(_take)/gather | solution.py:22
  144.7 12.8 %convolution_multiply_fusion.4 = f32[128,128,256]{2,1,0:T(8,128)} fusion(f32[128]{0:T(128)S(1)} %get-tuple-element.384, bf16[128,128,256]{2,1,0:T(8,128)(2,1)} %gather_fusion, pred[128]{0:T(512)(128)(4,1)S(1)} %get-tuple-element.386, bf16[512,128,128]{2,1,0:T(8,128)(2,1)} %get-tuple-element.422, s32[]{:T(128)S(6)} %select_n.85), kind=kOutput, calls=%fused_computation.4.clone.1 | convolution fusion | flops 1082130432 | bytes 29360772 | tf_op jit(solution)/shard_map/while/body/eval_jaxpr/tab,tbf->taf/dot_general | solution.py:23
  157.5 0.1 compare_select_fusion.8
  157.6 24.3 %scatter_fusion = f32[16,128,256]{2,1,0:T(8,128)S(1)} fusion(f32[16,128,256]{2,1,0:T(8,128)S(1)} %get-tuple-element.409, s32[128]{0:T(128)S(1)} %compare_select_fusion.8, f32[128,128,256]{2,1,0:T(8,128)} %convolution_multiply_fusion.4), kind=kCustom, calls=%fused_computation.2.clone.1 | custom fusion | flops 4194304 | bytes 50332160 | tf_op jit(solution)/shard_map/while/body/eval_jaxpr/scatter-add | solution.py:27
  181.9 0.1 compare_and_fusion.4
  182.0 8.2 %gather_fusion = bf16[128,128,256]{2,1,0:T(8,128)(2,1)} fusion(bf16[32,128,256]{2,1,0:T(8,128)(2,1)} %get-tuple-element.424, s32[1024]{0:T(1024)S(1)} %pad_clamp_fusion.4), kind=kCustom, calls=%fused_computation.clone.1 | custom fusion | bytes 16777728 | tf_op jit(solution)/shard_map/while/body/eval_jaxpr/jit(_take)/gather | solution.py:22
  190.2 12.8 %convolution_multiply_fusion.4 = f32[128,128,256]{2,1,0:T(8,128)} fusion(f32[128]{0:T(128)S(1)} %get-tuple-element.384, bf16[128,128,256]{2,1,0:T(8,128)(2,1)} %gather_fusion, pred[128]{0:T(512)(128)(4,1)S(1)} %get-tuple-element.386, bf16[512,128,128]{2,1,0:T(8,128)(2,1)} %get-tuple-element.422, s32[]{:T(128)S(6)} %select_n.85), kind=kOutput, calls=%fused_computation.4.clone.1 | convolution fusion | flops 1082130432 | bytes 29360772 | tf_op jit(solution)/shard_map/while/body/eval_jaxpr/tab,tbf->taf/dot_general | solution.py:23
  203.0 0.1 compare_select_fusion.8
  203.1 24.3 %scatter_fusion = f32[16,128,256]{2,1,0:T(8,128)S(1)} fusion(f32[16,128,256]{2,1,0:T(8,128)S(1)} %get-tuple-element.409, s32[128]{0:T(128)S(1)} %compare_select_fusion.8, f32[128,128,256]{2,1,0:T(8,128)} %convolution_multiply_fusion.4), kind=kCustom, calls=%fused_computation.2.clone.1 | custom fusion | flops 4194304 | bytes 50332160 | tf_op jit(solution)/shard_map/while/body/eval_jaxpr/scatter-add | solution.py:27
  227.4 1.3 copy-done.1
  228.7 0.0 reduce-scatter.3.cloned.1.call-update
  228.7 0.0 all-gather.5.cloned.1.call-start
  228.8 34.6 %reduce-scatter.3.cloned.1.call-done = f32[512,256]{1,0:T(8,128)} async-done(((f32[2048,256]{1,0:T(8,128)}), f32[512,256]{1,0:T(8,128)}) %reduce-scatter.3.cloned.1.call-update) | async-done | bytes 524304 | tf_op jit(solution)/shard_map/reduce_scatter | solution.py:49
  263.4 2.1 multiply_convert_fusion
  265.5 0.0 all-gather.5.cloned.1.call-update
  265.5 0.2 reduce-scatter.5.cloned.1.call-start
  265.7 22.4 %copy.10 = bf16[1,1,512,128,128]{3,4,2,1,0:T(8,128)(2,1)} copy(bf16[1,1,512,128,128]{4,3,2,1,0:T(8,128)(2,1)} %bitcast.21) | data formatting | bytes 33554432 | tf_op args[5]
  288.1 4.3 all-gather.5.cloned.1.call-done
  292.4 2.4 broadcast_in_dim.75
  294.8 234.0 %while.27 = (s32[]{:T(128)}, f32[32,128,256]{2,1,0:T(8,128)}, s32[512]{0:T(512)S(1)}, bf16[512,128,128]{1,2,0:T(8,128)(2,1)}, s32[512]{0:T(512)S(1)}, /*index=5*...) while((s32[]{:T(128)}, f32[32,128,256]{2,1,0:T(8,128)}, ...), condition=%wide.region_6.7_spmd, body=%wide.region_4.6_spmd.sunk | while | flops 1086327040 | bytes 96478248 | solution.py:30
  294.8 0.1 compare_and_fusion.5
  294.9 7.8 %gather_fusion.1 = bf16[128,128,256]{2,1,0:T(8,128)(2,1)} fusion(bf16[16,128,256]{2,1,0:T(8,128)(2,1)} %get-tuple-element.457, s32[1024]{0:T(1024)S(1)} %pad_clamp_fusion.5), kind=kCustom, calls=%fused_computation.1.clone.1 | custom fusion | bytes 16777728 | tf_op jit(solution)/shard_map/while/body/eval_jaxpr/jit(_take)/gather | solution.py:22
  302.7 12.8 %convolution_multiply_fusion.5 = f32[128,128,256]{2,1,0:T(8,128)} fusion(f32[128]{0:T(128)S(1)} %get-tuple-element.394, bf16[128,128,256]{2,1,0:T(8,128)(2,1)} %gather_fusion.1, pred[128]{0:T(512)(128)(4,1)S(1)} %get-tuple-element.396, bf16[512,128,128]{1,2,0:T(8,128)(2,1)} %get-tuple-element.455, s32[]{:T(128)S(6)} %select_n.88), kind=kOutput, calls=%fused_computation.16.clone.1 | convolution fusion | flops 1082130432 | bytes 29360772 | tf_op jit(solution)/shard_map/while/body/eval_jaxpr/tba,tbf->taf/dot_general | solution.py:23
  315.5 0.1 compare_select_fusion.9
  315.5 37.9 %scatter_fusion.1 = f32[32,128,256]{2,1,0:T(8,128)} fusion(f32[32,128,256]{2,1,0:T(8,128)} %get-tuple-element.442, s32[128]{0:T(128)S(1)} %compare_select_fusion.9, f32[128,128,256]{2,1,0:T(8,128)} %convolution_multiply_fusion.5), kind=kCustom, calls=%fused_computation.3.clone.1 | custom fusion | flops 4194304 | bytes 50332160 | tf_op jit(solution)/shard_map/while/body/eval_jaxpr/scatter-add | solution.py:27
  353.4 0.1 compare_and_fusion.5
  353.5 7.8 %gather_fusion.1 = bf16[128,128,256]{2,1,0:T(8,128)(2,1)} fusion(bf16[16,128,256]{2,1,0:T(8,128)(2,1)} %get-tuple-element.457, s32[1024]{0:T(1024)S(1)} %pad_clamp_fusion.5), kind=kCustom, calls=%fused_computation.1.clone.1 | custom fusion | bytes 16777728 | tf_op jit(solution)/shard_map/while/body/eval_jaxpr/jit(_take)/gather | solution.py:22
  361.2 12.8 %convolution_multiply_fusion.5 = f32[128,128,256]{2,1,0:T(8,128)} fusion(f32[128]{0:T(128)S(1)} %get-tuple-element.394, bf16[128,128,256]{2,1,0:T(8,128)(2,1)} %gather_fusion.1, pred[128]{0:T(512)(128)(4,1)S(1)} %get-tuple-element.396, bf16[512,128,128]{1,2,0:T(8,128)(2,1)} %get-tuple-element.455, s32[]{:T(128)S(6)} %select_n.88), kind=kOutput, calls=%fused_computation.16.clone.1 | convolution fusion | flops 1082130432 | bytes 29360772 | tf_op jit(solution)/shard_map/while/body/eval_jaxpr/tba,tbf->taf/dot_general | solution.py:23
  374.0 0.1 compare_select_fusion.9
  374.1 37.7 %scatter_fusion.1 = f32[32,128,256]{2,1,0:T(8,128)} fusion(f32[32,128,256]{2,1,0:T(8,128)} %get-tuple-element.442, s32[128]{0:T(128)S(1)} %compare_select_fusion.9, f32[128,128,256]{2,1,0:T(8,128)} %convolution_multiply_fusion.5), kind=kCustom, calls=%fused_computation.3.clone.1 | custom fusion | flops 4194304 | bytes 50332160 | tf_op jit(solution)/shard_map/while/body/eval_jaxpr/scatter-add | solution.py:27
  411.8 0.1 compare_and_fusion.5
  411.9 7.8 %gather_fusion.1 = bf16[128,128,256]{2,1,0:T(8,128)(2,1)} fusion(bf16[16,128,256]{2,1,0:T(8,128)(2,1)} %get-tuple-element.457, s32[1024]{0:T(1024)S(1)} %pad_clamp_fusion.5), kind=kCustom, calls=%fused_computation.1.clone.1 | custom fusion | bytes 16777728 | tf_op jit(solution)/shard_map/while/body/eval_jaxpr/jit(_take)/gather | solution.py:22
  419.7 12.8 %convolution_multiply_fusion.5 = f32[128,128,256]{2,1,0:T(8,128)} fusion(f32[128]{0:T(128)S(1)} %get-tuple-element.394, bf16[128,128,256]{2,1,0:T(8,128)(2,1)} %gather_fusion.1, pred[128]{0:T(512)(128)(4,1)S(1)} %get-tuple-element.396, bf16[512,128,128]{1,2,0:T(8,128)(2,1)} %get-tuple-element.455, s32[]{:T(128)S(6)} %select_n.88), kind=kOutput, calls=%fused_computation.16.clone.1 | convolution fusion | flops 1082130432 | bytes 29360772 | tf_op jit(solution)/shard_map/while/body/eval_jaxpr/tba,tbf->taf/dot_general | solution.py:23
  432.5 0.1 compare_select_fusion.9
  432.6 37.6 %scatter_fusion.1 = f32[32,128,256]{2,1,0:T(8,128)} fusion(f32[32,128,256]{2,1,0:T(8,128)} %get-tuple-element.442, s32[128]{0:T(128)S(1)} %compare_select_fusion.9, f32[128,128,256]{2,1,0:T(8,128)} %convolution_multiply_fusion.5), kind=kCustom, calls=%fused_computation.3.clone.1 | custom fusion | flops 4194304 | bytes 50332160 | tf_op jit(solution)/shard_map/while/body/eval_jaxpr/scatter-add | solution.py:27
  470.2 0.1 compare_and_fusion.5
  470.3 7.8 %gather_fusion.1 = bf16[128,128,256]{2,1,0:T(8,128)(2,1)} fusion(bf16[16,128,256]{2,1,0:T(8,128)(2,1)} %get-tuple-element.457, s32[1024]{0:T(1024)S(1)} %pad_clamp_fusion.5), kind=kCustom, calls=%fused_computation.1.clone.1 | custom fusion | bytes 16777728 | tf_op jit(solution)/shard_map/while/body/eval_jaxpr/jit(_take)/gather | solution.py:22
  478.0 12.8 %convolution_multiply_fusion.5 = f32[128,128,256]{2,1,0:T(8,128)} fusion(f32[128]{0:T(128)S(1)} %get-tuple-element.394, bf16[128,128,256]{2,1,0:T(8,128)(2,1)} %gather_fusion.1, pred[128]{0:T(512)(128)(4,1)S(1)} %get-tuple-element.396, bf16[512,128,128]{1,2,0:T(8,128)(2,1)} %get-tuple-element.455, s32[]{:T(128)S(6)} %select_n.88), kind=kOutput, calls=%fused_computation.16.clone.1 | convolution fusion | flops 1082130432 | bytes 29360772 | tf_op jit(solution)/shard_map/while/body/eval_jaxpr/tba,tbf->taf/dot_general | solution.py:23
  490.8 0.1 compare_select_fusion.9
  490.9 37.9 %scatter_fusion.1 = f32[32,128,256]{2,1,0:T(8,128)} fusion(f32[32,128,256]{2,1,0:T(8,128)} %get-tuple-element.442, s32[128]{0:T(128)S(1)} %compare_select_fusion.9, f32[128,128,256]{2,1,0:T(8,128)} %convolution_multiply_fusion.5), kind=kCustom, calls=%fused_computation.3.clone.1 | custom fusion | flops 4194304 | bytes 50332160 | tf_op jit(solution)/shard_map/while/body/eval_jaxpr/scatter-add | solution.py:27
  528.8 0.0 all-reduce.2.cloned.1.call-start
  528.8 50.8 %reduce-scatter.5.cloned.1.call-done = f32[512,256]{1,0:T(8,128)} async-done(((f32[4096,256]{1,0:T(8,128)}), f32[512,256]{1,0:T(8,128)}) %reduce-scatter.5.cloned.1.call-update) | async-done | bytes 524304 | tf_op jit(solution)/shard_map/reduce_scatter | solution.py:63
  579.6 2.0 convolution_bitcast_fusion
  581.6 2.0 convolution_convert_fusion.1
  583.7 127.0 %all-reduce.2.cloned.1.call-done = f32[256,256]{0,1:T(8,128)} async-done(((f32[256,256]{0,1:T(8,128)}), f32[256,256]{0,1:T(8,128)}) %all-reduce.2.cloned.1.call-update) | async-done | bytes 262160 | tf_op jit(solution)/shard_map/psum | solution.py:70
  710.6 1.8 copy.12
  (22 shorter events, 0.1 us)
Async XLA Ops:
  7.2 34.4 %copy-start = (bf16[256,256]{1,0:T(8,128)(2,1)S(1)}, bf16[256,256]{1,0:T(8,128)(2,1)}, u32[]{:S(2)}) copy-start(bf16[256,256]{1,0:T(8,128)(2,1)} %param.12) | copy-start | bytes 393220
  7.2 38.2 %copy-start.4 = (s32[1,1,512]{2,1,0:T(1,128)S(1)}, s32[1,1,512]{2,1,0:T(1,128)}, u32[]{:S(2)}) copy-start(s32[1,1,512]{2,1,0:T(1,128)} %param.14) | copy-start | bytes 6148
  7.2 38.2 %copy-start.5 = (s32[1,1,512]{2,1,0:T(1,128)S(1)}, s32[1,1,512]{2,1,0:T(1,128)}, u32[]{:S(2)}) copy-start(s32[1,1,512]{2,1,0:T(1,128)} %param.15) | copy-start | bytes 6148
  7.2 34.3 %all-gather.3.cloned.1.call-start = ((), (), s32[]{:S(2)}) async-start(), calls=%async_computation.2 | async-start | bytes 2359296 | tf_op jit(solution)/shard_map/all_gather | solution.py:44
  7.9 255.5 %reduce-scatter.3.cloned.1.call-start = ((), (), s32[]{:S(2)}) async-start(), calls=%async_computation.3 | async-start | bytes 2621440 | tf_op jit(solution)/shard_map/reduce_scatter | solution.py:49
  45.4 218.0 %copy-start.3 = (bf16[512,256]{1,0:T(8,128)(2,1)S(1)}, bf16[512,256]{1,0:T(8,128)(2,1)}, u32[]{:S(2)}) copy-start(bf16[512,256]{1,0:T(8,128)(2,1)} %param.13) | copy-start | bytes 786436
  227.4 1.3 copy-start.1
  228.7 63.6 %all-gather.5.cloned.1.call-start = ((), (), s32[]{:S(2)}) async-start(), calls=%async_computation.4 | async-start | bytes 1310720 | tf_op jit(solution)/shard_map/all_gather | solution.py:52
  265.5 314.1 %reduce-scatter.5.cloned.1.call-start = ((), (), s32[]{:S(2)}) async-start(), calls=%async_computation.5 | async-start | bytes 4718592 | tf_op jit(solution)/shard_map/reduce_scatter | solution.py:63
  294.8 284.8 %copy-start.2 = (bf16[512,256]{1,0:T(8,128)(2,1)S(1)}, bf16[512,256]{1,0:T(8,128)(2,1)}, u32[]{:S(2)}) copy-start(bf16[512,256]{1,0:T(8,128)(2,1)} %param.11) | copy-start | bytes 786436
  528.8 181.8 %all-reduce.2.cloned.1.call-start = ((), (), s32[]{:S(2)}) async-start(), calls=%async_computation.6 | async-start | bytes 524288 | tf_op jit(solution)/shard_map/psum | solution.py:70
Sparse Core Ops, SparseCore 0:
  9.6 31.8 all-gather.2
  228.9 34.4 reduce-scatter.2
  265.8 26.4 all-gather.4
  528.9 50.6 reduce-scatter.4
  585.5 125.0 all-reduce.1
where the time goes:
time: 721 us; the launch traced here: 719 us
  other arithmetic  252 us (35%)
  waiting for transfers between devices  250 us (35%)
  matrix products  110 us (15%)
  local copies, waits for them, and re-layouts  91.8 us (13%)
  between operations  14.5 us (2%)
    scatter-add x8, other arithmetic, accumulate(): return summed.at[places].add(products)  248 us
    psum x1, waiting for transfers between devices, body(): grad_weight = lax.psum(local_weight, ('dom', 'rep'))  127 us
    dot_general x8, matrix products, accumulate(): jnp.einsum(pattern, block_values, picked, preferred_element_type=jnp.floa...  103 us
    gather x8, local copies, waits for them, and re-layouts, accumulate(): picked = jnp.take(source, picks, axis=0)  63.7 us
    reduce_scatter x1, waiting for transfers between devices, body(): lax.psum_scatter(back_partial, 'dom', scatter_dimension=0, tiled=True)  50.8 us
    reduce_scatter x1, waiting for transfers between devices, body(): lax.psum_scatter(partial_value, 'rep', scatter_dimension=0, tiled=True)  34.6 us
    all_gather x1, waiting for transfers between devices, body(): raw_rows = lax.all_gather(node_features, 'dom', axis=0, tiled=True)  32.9 us
    unnamed x14, local copies, waits for them, and re-layouts  25.5 us
  transfers between devices with their start and end apart: 5, of which 5 were waited for; matrix products, arithmetic and copies ran while one was open for 3% of the time, Pallas kernels for 0%

commit v1 on v0

--- a/solution.py
+++ b/solution.py
@@ -67,7 +67,7 @@
         jnp.bfloat16
     )
     local_weight = jnp.dot(node_features.T, grad_projected, preferred_element_type=jnp.float32)
-    grad_weight = lax.psum(local_weight, ("dom", "rep"))
+    grad_weight = lax.psum(lax.psum(local_weight, "rep"), "dom")
     return (output, grad_features, grad_weight)
 
 

time: 721 us -> 693 us (0.961)
  waiting for transfers between devices: 250 us -> 222 us
    psum x1 -> x2, waiting for transfers between devices: 127 us -> 98.4 us  [body(): grad_weight = lax.psum(lax.psum(local_weight, 'rep'), 'dom')]
  transfers between devices with their start and end apart: 5 -> 6, of which waited for: 5 -> 6; matrix products, arithmetic and copies ran while one was open for 3% -> 4% of each run, Pallas kernels for 0% -> 0%
where the time goes in v1:
time: 693 us; the launch traced here: 691 us
  other arithmetic  252 us (36%)
  waiting for transfers between devices  222 us (32%)
  matrix products  110 us (16%)
  local copies, waits for them, and re-layouts  91.8 us (13%)
  between operations  14.8 us (2%)
    scatter-add x8, other arithmetic, accumulate(): return summed.at[places].add(products)  248 us
    dot_general x8, matrix products, accumulate(): jnp.einsum(pattern, block_values, picked, preferred_element_type=jnp.floa...  103 us
    psum x2, waiting for transfers between devices, body(): grad_weight = lax.psum(lax.psum(local_weight, 'rep'), 'dom')  98.4 us
    gather x8, local copies, waits for them, and re-layouts, accumulate(): picked = jnp.take(source, picks, axis=0)  63.7 us
    reduce_scatter x1, waiting for transfers between devices, body(): lax.psum_scatter(back_partial, 'dom', scatter_dimension=0, tiled=True)  50.8 us
    reduce_scatter x1, waiting for transfers between devices, body(): lax.psum_scatter(partial_value, 'rep', scatter_dimension=0, tiled=True)  34.6 us
    all_gather x1, waiting for transfers between devices, body(): raw_rows = lax.all_gather(node_features, 'dom', axis=0, tiled=True)  32.9 us
    unnamed x14, local copies, waits for them, and re-layouts  25.5 us
  transfers between devices with their start and end apart: 6, of which 6 were waited for; matrix products, arithmetic and copies ran while one was open for 4% of the time, Pallas kernels for 0%

profile of v1, /device:TPU:0, one launch (start us, length us, event | category | flops | bytes accessed | tf_op | source)
XLA Modules:
  0.0 690.8 jit_solution(9641742613589210749)
XLA Ops:
  7.2 0.0 all-gather.3.cloned.1.call-start
  7.2 0.7 all-gather.3.cloned.1.call-update
  7.9 0.0 reduce-scatter.3.cloned.1.call-start
  8.6 32.9 %all-gather.3.cloned.1.call-done = bf16[4096,256]{1,0:T(8,128)(2,1)} async-done(((bf16[512,256]{1,0:T(8,128)(2,1)}), bf16[4096,256]{1,0:T(8,128)(2,1)}) %all-gather.3.cloned.1.call-update) | async-done | bytes 2097168 | tf_op jit(solution)/shard_map/all_gather | solution.py:44
  41.5 3.7 convolution_convert_fusion
  45.2 0.2 broadcast_in_dim.74
  45.4 181.9 %while.26 = (s32[]{:T(128)}, f32[16,128,256]{2,1,0:T(8,128)S(1)}, s32[512]{0:T(512)S(1)}, bf16[512,128,128]{2,1,0:T(8,128)(2,1)}, s32[512]{0:T(512)S(1)}, /*inde...) while((s32[]{:T(128)}, f32[16,128,256]{2,1,0:T(8,128)S(1)}, ...), condition=%wide.region_2.3_spmd, body=%wide.region_0.2_spmd.sunk | while | flops 1086327040 | bytes 96478248 | solution.py:30
  45.4 0.1 compare_and_fusion.4
  45.5 8.2 %gather_fusion = bf16[128,128,256]{2,1,0:T(8,128)(2,1)} fusion(bf16[32,128,256]{2,1,0:T(8,128)(2,1)} %get-tuple-element.424, s32[1024]{0:T(1024)S(1)} %pad_clamp_fusion.4), kind=kCustom, calls=%fused_computation.clone.1 | custom fusion | bytes 16777728 | tf_op jit(solution)/shard_map/while/body/eval_jaxpr/jit(_take)/gather | solution.py:22
  53.7 12.8 %convolution_multiply_fusion.4 = f32[128,128,256]{2,1,0:T(8,128)} fusion(f32[128]{0:T(128)S(1)} %get-tuple-element.384, bf16[128,128,256]{2,1,0:T(8,128)(2,1)} %gather_fusion, pred[128]{0:T(512)(128)(4,1)S(1)} %get-tuple-element.386, bf16[512,128,128]{2,1,0:T(8,128)(2,1)} %get-tuple-element.422, s32[]{:T(128)S(6)} %select_n.85), kind=kOutput, calls=%fused_computation.4.clone.1 | convolution fusion | flops 1082130432 | bytes 29360772 | tf_op jit(solution)/shard_map/while/body/eval_jaxpr/tab,tbf->taf/dot_general | solution.py:23
  66.5 0.1 compare_select_fusion.8
  66.6 24.3 %scatter_fusion = f32[16,128,256]{2,1,0:T(8,128)S(1)} fusion(f32[16,128,256]{2,1,0:T(8,128)S(1)} %get-tuple-element.409, s32[128]{0:T(128)S(1)} %compare_select_fusion.8, f32[128,128,256]{2,1,0:T(8,128)} %convolution_multiply_fusion.4), kind=kCustom, calls=%fused_computation.2.clone.1 | custom fusion | flops 4194304 | bytes 50332160 | tf_op jit(solution)/shard_map/while/body/eval_jaxpr/scatter-add | solution.py:27
  90.9 0.1 compare_and_fusion.4
  91.0 8.2 %gather_fusion = bf16[128,128,256]{2,1,0:T(8,128)(2,1)} fusion(bf16[32,128,256]{2,1,0:T(8,128)(2,1)} %get-tuple-element.424, s32[1024]{0:T(1024)S(1)} %pad_clamp_fusion.4), kind=kCustom, calls=%fused_computation.clone.1 | custom fusion | bytes 16777728 | tf_op jit(solution)/shard_map/while/body/eval_jaxpr/jit(_take)/gather | solution.py:22
  99.2 12.8 %convolution_multiply_fusion.4 = f32[128,128,256]{2,1,0:T(8,128)} fusion(f32[128]{0:T(128)S(1)} %get-tuple-element.384, bf16[128,128,256]{2,1,0:T(8,128)(2,1)} %gather_fusion, pred[128]{0:T(512)(128)(4,1)S(1)} %get-tuple-element.386, bf16[512,128,128]{2,1,0:T(8,128)(2,1)} %get-tuple-element.422, s32[]{:T(128)S(6)} %select_n.85), kind=kOutput, calls=%fused_computation.4.clone.1 | convolution fusion | flops 1082130432 | bytes 29360772 | tf_op jit(solution)/shard_map/while/body/eval_jaxpr/tab,tbf->taf/dot_general | solution.py:23
  112.0 0.1 compare_select_fusion.8
  112.1 24.3 %scatter_fusion = f32[16,128,256]{2,1,0:T(8,128)S(1)} fusion(f32[16,128,256]{2,1,0:T(8,128)S(1)} %get-tuple-element.409, s32[128]{0:T(128)S(1)} %compare_select_fusion.8, f32[128,128,256]{2,1,0:T(8,128)} %convolution_multiply_fusion.4), kind=kCustom, calls=%fused_computation.2.clone.1 | custom fusion | flops 4194304 | bytes 50332160 | tf_op jit(solution)/shard_map/while/body/eval_jaxpr/scatter-add | solution.py:27
  136.4 0.1 compare_and_fusion.4
  136.5 8.2 %gather_fusion = bf16[128,128,256]{2,1,0:T(8,128)(2,1)} fusion(bf16[32,128,256]{2,1,0:T(8,128)(2,1)} %get-tuple-element.424, s32[1024]{0:T(1024)S(1)} %pad_clamp_fusion.4), kind=kCustom, calls=%fused_computation.clone.1 | custom fusion | bytes 16777728 | tf_op jit(solution)/shard_map/while/body/eval_jaxpr/jit(_take)/gather | solution.py:22
  144.7 12.8 %convolution_multiply_fusion.4 = f32[128,128,256]{2,1,0:T(8,128)} fusion(f32[128]{0:T(128)S(1)} %get-tuple-element.384, bf16[128,128,256]{2,1,0:T(8,128)(2,1)} %gather_fusion, pred[128]{0:T(512)(128)(4,1)S(1)} %get-tuple-element.386, bf16[512,128,128]{2,1,0:T(8,128)(2,1)} %get-tuple-element.422, s32[]{:T(128)S(6)} %select_n.85), kind=kOutput, calls=%fused_computation.4.clone.1 | convolution fusion | flops 1082130432 | bytes 29360772 | tf_op jit(solution)/shard_map/while/body/eval_jaxpr/tab,tbf->taf/dot_general | solution.py:23
  157.5 0.1 compare_select_fusion.8
  157.6 24.3 %scatter_fusion = f32[16,128,256]{2,1,0:T(8,128)S(1)} fusion(f32[16,128,256]{2,1,0:T(8,128)S(1)} %get-tuple-element.409, s32[128]{0:T(128)S(1)} %compare_select_fusion.8, f32[128,128,256]{2,1,0:T(8,128)} %convolution_multiply_fusion.4), kind=kCustom, calls=%fused_computation.2.clone.1 | custom fusion | flops 4194304 | bytes 50332160 | tf_op jit(solution)/shard_map/while/body/eval_jaxpr/scatter-add | solution.py:27
  181.9 0.1 compare_and_fusion.4
  182.0 8.2 %gather_fusion = bf16[128,128,256]{2,1,0:T(8,128)(2,1)} fusion(bf16[32,128,256]{2,1,0:T(8,128)(2,1)} %get-tuple-element.424, s32[1024]{0:T(1024)S(1)} %pad_clamp_fusion.4), kind=kCustom, calls=%fused_computation.clone.1 | custom fusion | bytes 16777728 | tf_op jit(solution)/shard_map/while/body/eval_jaxpr/jit(_take)/gather | solution.py:22
  190.2 12.8 %convolution_multiply_fusion.4 = f32[128,128,256]{2,1,0:T(8,128)} fusion(f32[128]{0:T(128)S(1)} %get-tuple-element.384, bf16[128,128,256]{2,1,0:T(8,128)(2,1)} %gather_fusion, pred[128]{0:T(512)(128)(4,1)S(1)} %get-tuple-element.386, bf16[512,128,128]{2,1,0:T(8,128)(2,1)} %get-tuple-element.422, s32[]{:T(128)S(6)} %select_n.85), kind=kOutput, calls=%fused_computation.4.clone.1 | convolution fusion | flops 1082130432 | bytes 29360772 | tf_op jit(solution)/shard_map/while/body/eval_jaxpr/tab,tbf->taf/dot_general | solution.py:23
  203.0 0.1 compare_select_fusion.8
  203.1 24.3 %scatter_fusion = f32[16,128,256]{2,1,0:T(8,128)S(1)} fusion(f32[16,128,256]{2,1,0:T(8,128)S(1)} %get-tuple-element.409, s32[128]{0:T(128)S(1)} %compare_select_fusion.8, f32[128,128,256]{2,1,0:T(8,128)} %convolution_multiply_fusion.4), kind=kCustom, calls=%fused_computation.2.clone.1 | custom fusion | flops 4194304 | bytes 50332160 | tf_op jit(solution)/shard_map/while/body/eval_jaxpr/scatter-add | solution.py:27
  227.4 1.3 copy-done.1
  228.7 0.0 all-gather.5.cloned.1.call-start
  228.8 34.6 %reduce-scatter.3.cloned.1.call-done = f32[512,256]{1,0:T(8,128)} async-done(((f32[2048,256]{1,0:T(8,128)}), f32[512,256]{1,0:T(8,128)}) %reduce-scatter.3.cloned.1.call-update) | async-done | bytes 524304 | tf_op jit(solution)/shard_map/reduce_scatter | solution.py:49
  263.4 2.1 multiply_convert_fusion
  265.5 0.2 reduce-scatter.5.cloned.1.call-start
  265.7 22.4 %copy.10 = bf16[1,1,512,128,128]{3,4,2,1,0:T(8,128)(2,1)} copy(bf16[1,1,512,128,128]{4,3,2,1,0:T(8,128)(2,1)} %bitcast.21) | data formatting | bytes 33554432 | tf_op args[5]
  288.1 4.3 all-gather.5.cloned.1.call-done
  292.4 2.4 broadcast_in_dim.75
  294.8 234.0 %while.27 = (s32[]{:T(128)}, f32[32,128,256]{2,1,0:T(8,128)}, s32[512]{0:T(512)S(1)}, bf16[512,128,128]{1,2,0:T(8,128)(2,1)}, s32[512]{0:T(512)S(1)}, /*index=5*...) while((s32[]{:T(128)}, f32[32,128,256]{2,1,0:T(8,128)}, ...), condition=%wide.region_6.7_spmd, body=%wide.region_4.6_spmd.sunk | while | flops 1086327040 | bytes 96478248 | solution.py:30
  294.8 0.1 compare_and_fusion.5
  294.9 7.8 %gather_fusion.1 = bf16[128,128,256]{2,1,0:T(8,128)(2,1)} fusion(bf16[16,128,256]{2,1,0:T(8,128)(2,1)} %get-tuple-element.457, s32[1024]{0:T(1024)S(1)} %pad_clamp_fusion.5), kind=kCustom, calls=%fused_computation.1.clone.1 | custom fusion | bytes 16777728 | tf_op jit(solution)/shard_map/while/body/eval_jaxpr/jit(_take)/gather | solution.py:22
  302.7 12.8 %convolution_multiply_fusion.5 = f32[128,128,256]{2,1,0:T(8,128)} fusion(f32[128]{0:T(128)S(1)} %get-tuple-element.394, bf16[128,128,256]{2,1,0:T(8,128)(2,1)} %gather_fusion.1, pred[128]{0:T(512)(128)(4,1)S(1)} %get-tuple-element.396, bf16[512,128,128]{1,2,0:T(8,128)(2,1)} %get-tuple-element.455, s32[]{:T(128)S(6)} %select_n.88), kind=kOutput, calls=%fused_computation.16.clone.1 | convolution fusion | flops 1082130432 | bytes 29360772 | tf_op jit(solution)/shard_map/while/body/eval_jaxpr/tba,tbf->taf/dot_general | solution.py:23
  315.5 0.1 compare_select_fusion.9
  315.5 37.9 %scatter_fusion.1 = f32[32,128,256]{2,1,0:T(8,128)} fusion(f32[32,128,256]{2,1,0:T(8,128)} %get-tuple-element.442, s32[128]{0:T(128)S(1)} %compare_select_fusion.9, f32[128,128,256]{2,1,0:T(8,128)} %convolution_multiply_fusion.5), kind=kCustom, calls=%fused_computation.3.clone.1 | custom fusion | flops 4194304 | bytes 50332160 | tf_op jit(solution)/shard_map/while/body/eval_jaxpr/scatter-add | solution.py:27
  353.4 0.1 compare_and_fusion.5
  353.5 7.8 %gather_fusion.1 = bf16[128,128,256]{2,1,0:T(8,128)(2,1)} fusion(bf16[16,128,256]{2,1,0:T(8,128)(2,1)} %get-tuple-element.457, s32[1024]{0:T(1024)S(1)} %pad_clamp_fusion.5), kind=kCustom, calls=%fused_computation.1.clone.1 | custom fusion | bytes 16777728 | tf_op jit(solution)/shard_map/while/body/eval_jaxpr/jit(_take)/gather | solution.py:22
  361.2 12.8 %convolution_multiply_fusion.5 = f32[128,128,256]{2,1,0:T(8,128)} fusion(f32[128]{0:T(128)S(1)} %get-tuple-element.394, bf16[128,128,256]{2,1,0:T(8,128)(2,1)} %gather_fusion.1, pred[128]{0:T(512)(128)(4,1)S(1)} %get-tuple-element.396, bf16[512,128,128]{1,2,0:T(8,128)(2,1)} %get-tuple-element.455, s32[]{:T(128)S(6)} %select_n.88), kind=kOutput, calls=%fused_computation.16.clone.1 | convolution fusion | flops 1082130432 | bytes 29360772 | tf_op jit(solution)/shard_map/while/body/eval_jaxpr/tba,tbf->taf/dot_general | solution.py:23
  374.0 0.1 compare_select_fusion.9
  374.1 37.7 %scatter_fusion.1 = f32[32,128,256]{2,1,0:T(8,128)} fusion(f32[32,128,256]{2,1,0:T(8,128)} %get-tuple-element.442, s32[128]{0:T(128)S(1)} %compare_select_fusion.9, f32[128,128,256]{2,1,0:T(8,128)} %convolution_multiply_fusion.5), kind=kCustom, calls=%fused_computation.3.clone.1 | custom fusion | flops 4194304 | bytes 50332160 | tf_op jit(solution)/shard_map/while/body/eval_jaxpr/scatter-add | solution.py:27
  411.8 0.1 compare_and_fusion.5
  411.9 7.8 %gather_fusion.1 = bf16[128,128,256]{2,1,0:T(8,128)(2,1)} fusion(bf16[16,128,256]{2,1,0:T(8,128)(2,1)} %get-tuple-element.457, s32[1024]{0:T(1024)S(1)} %pad_clamp_fusion.5), kind=kCustom, calls=%fused_computation.1.clone.1 | custom fusion | bytes 16777728 | tf_op jit(solution)/shard_map/while/body/eval_jaxpr/jit(_take)/gather | solution.py:22
  419.7 12.8 %convolution_multiply_fusion.5 = f32[128,128,256]{2,1,0:T(8,128)} fusion(f32[128]{0:T(128)S(1)} %get-tuple-element.394, bf16[128,128,256]{2,1,0:T(8,128)(2,1)} %gather_fusion.1, pred[128]{0:T(512)(128)(4,1)S(1)} %get-tuple-element.396, bf16[512,128,128]{1,2,0:T(8,128)(2,1)} %get-tuple-element.455, s32[]{:T(128)S(6)} %select_n.88), kind=kOutput, calls=%fused_computation.16.clone.1 | convolution fusion | flops 1082130432 | bytes 29360772 | tf_op jit(solution)/shard_map/while/body/eval_jaxpr/tba,tbf->taf/dot_general | solution.py:23
  432.5 0.1 compare_select_fusion.9
  432.6 37.6 %scatter_fusion.1 = f32[32,128,256]{2,1,0:T(8,128)} fusion(f32[32,128,256]{2,1,0:T(8,128)} %get-tuple-element.442, s32[128]{0:T(128)S(1)} %compare_select_fusion.9, f32[128,128,256]{2,1,0:T(8,128)} %convolution_multiply_fusion.5), kind=kCustom, calls=%fused_computation.3.clone.1 | custom fusion | flops 4194304 | bytes 50332160 | tf_op jit(solution)/shard_map/while/body/eval_jaxpr/scatter-add | solution.py:27
  470.2 0.1 compare_and_fusion.5
  470.3 7.8 %gather_fusion.1 = bf16[128,128,256]{2,1,0:T(8,128)(2,1)} fusion(bf16[16,128,256]{2,1,0:T(8,128)(2,1)} %get-tuple-element.457, s32[1024]{0:T(1024)S(1)} %pad_clamp_fusion.5), kind=kCustom, calls=%fused_computation.1.clone.1 | custom fusion | bytes 16777728 | tf_op jit(solution)/shard_map/while/body/eval_jaxpr/jit(_take)/gather | solution.py:22
  478.0 12.8 %convolution_multiply_fusion.5 = f32[128,128,256]{2,1,0:T(8,128)} fusion(f32[128]{0:T(128)S(1)} %get-tuple-element.394, bf16[128,128,256]{2,1,0:T(8,128)(2,1)} %gather_fusion.1, pred[128]{0:T(512)(128)(4,1)S(1)} %get-tuple-element.396, bf16[512,128,128]{1,2,0:T(8,128)(2,1)} %get-tuple-element.455, s32[]{:T(128)S(6)} %select_n.88), kind=kOutput, calls=%fused_computation.16.clone.1 | convolution fusion | flops 1082130432 | bytes 29360772 | tf_op jit(solution)/shard_map/while/body/eval_jaxpr/tba,tbf->taf/dot_general | solution.py:23
  490.8 0.1 compare_select_fusion.9
  490.9 37.9 %scatter_fusion.1 = f32[32,128,256]{2,1,0:T(8,128)} fusion(f32[32,128,256]{2,1,0:T(8,128)} %get-tuple-element.442, s32[128]{0:T(128)S(1)} %compare_select_fusion.9, f32[128,128,256]{2,1,0:T(8,128)} %convolution_multiply_fusion.5), kind=kCustom, calls=%fused_computation.3.clone.1 | custom fusion | flops 4194304 | bytes 50332160 | tf_op jit(solution)/shard_map/while/body/eval_jaxpr/scatter-add | solution.py:27
  528.8 0.0 all-reduce.3.cloned.1.call-start
  528.8 50.8 %reduce-scatter.5.cloned.1.call-done = f32[512,256]{1,0:T(8,128)} async-done(((f32[4096,256]{1,0:T(8,128)}), f32[512,256]{1,0:T(8,128)}) %reduce-scatter.5.cloned.1.call-update) | async-done | bytes 524304 | tf_op jit(solution)/shard_map/reduce_scatter | solution.py:63
  579.6 2.0 convolution_bitcast_fusion
  581.6 0.0 all-reduce.5.cloned.1.call-start
  581.7 42.8 %all-reduce.3.cloned.1.call-done = f32[256,256]{0,1:T(8,128)} async-done(((f32[256,256]{0,1:T(8,128)}), f32[256,256]{0,1:T(8,128)}) %all-reduce.3.cloned.1.call-update) | async-done | bytes 262160 | tf_op jit(solution)/shard_map/psum | solution.py:70
  624.5 2.0 convolution_convert_fusion.1
  626.6 55.6 %all-reduce.5.cloned.1.call-done = f32[256,256]{0,1:T(8,128)} async-done(((f32[256,256]{0,1:T(8,128)}), f32[256,256]{0,1:T(8,128)}) %all-reduce.5.cloned.1.call-update) | async-done | bytes 262160 | tf_op jit(solution)/shard_map/psum | solution.py:70
  682.1 1.8 copy.12
  (25 shorter events, 0.2 us)
Async XLA Ops:
  7.2 34.4 %copy-start = (bf16[256,256]{1,0:T(8,128)(2,1)S(1)}, bf16[256,256]{1,0:T(8,128)(2,1)}, u32[]{:S(2)}) copy-start(bf16[256,256]{1,0:T(8,128)(2,1)} %param.12) | copy-start | bytes 393220
  7.2 38.2 %copy-start.4 = (s32[1,1,512]{2,1,0:T(1,128)S(1)}, s32[1,1,512]{2,1,0:T(1,128)}, u32[]{:S(2)}) copy-start(s32[1,1,512]{2,1,0:T(1,128)} %param.14) | copy-start | bytes 6148
  7.2 38.2 %copy-start.5 = (s32[1,1,512]{2,1,0:T(1,128)S(1)}, s32[1,1,512]{2,1,0:T(1,128)}, u32[]{:S(2)}) copy-start(s32[1,1,512]{2,1,0:T(1,128)} %param.15) | copy-start | bytes 6148
  7.2 34.3 %all-gather.3.cloned.1.call-start = ((), (), s32[]{:S(2)}) async-start(), calls=%async_computation.2 | async-start | bytes 2359296 | tf_op jit(solution)/shard_map/all_gather | solution.py:44
  7.9 255.5 %reduce-scatter.3.cloned.1.call-start = ((), (), s32[]{:S(2)}) async-start(), calls=%async_computation.3 | async-start | bytes 2621440 | tf_op jit(solution)/shard_map/reduce_scatter | solution.py:49
  45.4 218.0 %copy-start.3 = (bf16[512,256]{1,0:T(8,128)(2,1)S(1)}, bf16[512,256]{1,0:T(8,128)(2,1)}, u32[]{:S(2)}) copy-start(bf16[512,256]{1,0:T(8,128)(2,1)} %param.13) | copy-start | bytes 786436
  227.4 1.3 copy-start.1
  228.7 63.6 %all-gather.5.cloned.1.call-start = ((), (), s32[]{:S(2)}) async-start(), calls=%async_computation.4 | async-start | bytes 1310720 | tf_op jit(solution)/shard_map/all_gather | solution.py:52
  265.5 314.1 %reduce-scatter.5.cloned.1.call-start = ((), (), s32[]{:S(2)}) async-start(), calls=%async_computation.5 | async-start | bytes 4718592 | tf_op jit(solution)/shard_map/reduce_scatter | solution.py:63
  294.8 284.8 %copy-start.2 = (bf16[512,256]{1,0:T(8,128)(2,1)S(1)}, bf16[512,256]{1,0:T(8,128)(2,1)}, u32[]{:S(2)}) copy-start(bf16[512,256]{1,0:T(8,128)(2,1)} %param.11) | copy-start | bytes 786436
  528.8 95.7 %all-reduce.3.cloned.1.call-start = ((), (), s32[]{:S(2)}) async-start(), calls=%async_computation.6 | async-start | bytes 524288 | tf_op jit(solution)/shard_map/psum | solution.py:70
  581.6 100.5 %all-reduce.5.cloned.1.call-start = ((), (), s32[]{:S(2)}) async-start(), calls=%async_computation.7 | async-start | bytes 524288 | tf_op jit(solution)/shard_map/psum | solution.py:70
Sparse Core Ops, SparseCore 0:
  9.6 31.8 all-gather.2
  228.9 34.4 reduce-scatter.2
  265.8 26.4 all-gather.4
  528.9 50.6 reduce-scatter.4
  583.0 41.5 all-reduce.2
  626.7 55.4 all-reduce.4
